TPU v7x, 256 devices: a whole 4x4x8 slice. The times are simulated.
256 devices in a mesh: dp: 32 (over x, z_hi, core), tensor: 8 (over y, z_lo).
Axes of the slice: x: 4, y: 4, z: 8 (z_hi: 4, z_lo: 2; z = z_hi * 2 + z_lo), core: 2. Of those that a mesh axis runs over, the one named last changes fastest.
Arguments:
- tokens: bfloat16 [64, 192, 4096], P('dp', None, 'tensor'), may hold values from -6 to 6
- grad_out: bfloat16 [64, 192, 4096], P('dp', None, 'tensor'), may hold values from -6 to 6
- counts: int32 [32], replicated, may hold values from 0 to 2, as said below
- gain: bfloat16 [4096], P('dp'), may hold values from 0.5 to 1.5
- wq: bfloat16 [4096, 4096], P('dp', 'tensor'), may hold values from -2.5 to 2.5
- wk: bfloat16 [4096, 1024], P('dp', 'tensor'), may hold values from -0.09375 to 0.09375
- wv: bfloat16 [4096, 1024], P('dp', 'tensor'), may hold values from -0.09375 to 0.09375
- wo: bfloat16 [4096, 4096], P('tensor', 'dp'), may hold values from -0.09375 to 0.09375
Outputs:
- mixed: bfloat16 [64, 192, 4096], P('dp', None, 'tensor')
- grad_tokens: bfloat16 [64, 192, 4096], P('dp', None, 'tensor')
- grad_gain: float32 [4096], P('dp')
- grad_wq: float32 [4096, 4096], P('dp', 'tensor')
- grad_wk: float32 [4096, 1024], P('dp', 'tensor')
- grad_wv: float32 [4096, 1024], P('dp', 'tensor')
- grad_wo: float32 [4096, 4096], P('tensor', 'dp')
Inputs may be any that keep to these rules, and one draw needn't show every extreme that they name: `counts`: replica r and replica r + 16 hold 2 live blocks together; in every draw some replica holds 2.
All inputs are finite; a program needn't handle non-finite values.
Results may differ from a plain program's by a relative error of at most 0.025.
Values may be sent and summed in bfloat16 or wider, within the bound.
No kernel may reach another device: no remote copies, remote signals or barrier semaphores. Data moves between devices by JAX's collectives and lax.ppermute only.
A program may use at most 128 MiB of HBM per device.

v0:
```python
import jax
import jax.numpy as jnp
from jax import lax
from jax.sharding import PartitionSpec as P

HEADS = 32
KV = 8
HD = 128


epsilon = 1e-05


def attention_forward(query_heads, key_heads, value_heads):
    length = query_heads.shape[1]
    score_scale = query_heads.shape[-1] ** (-0.5)
    position = jnp.arange(length)
    causal = position[None, :] <= position[:, None]
    scores = (
        jnp.einsum("btgrh,bugh->bgrtu", query_heads, key_heads, preferred_element_type=jnp.float32)
        * score_scale
    )
    scores = jnp.where(causal, scores, -1e30)
    row_max = jnp.max(scores, axis=-1, keepdims=True)
    exp_scores = jnp.exp(scores - row_max)
    softmax_out = exp_scores / jnp.sum(exp_scores, axis=-1, keepdims=True)
    softmax_low = softmax_out.astype(jnp.bfloat16)
    context = jnp.einsum(
        "bgrtu,bugh->btgrh", softmax_low, value_heads, preferred_element_type=jnp.float32
    ).astype(jnp.bfloat16)
    return (softmax_out, softmax_low, context)


def attention_backward(grad_context, query_heads, key_heads, value_heads, softmax_out, softmax_low):
    score_scale = query_heads.shape[-1] ** (-0.5)
    grad_soft = jnp.einsum(
        "btgrh,bugh->bgrtu", grad_context, value_heads, preferred_element_type=jnp.float32
    )
    row_inner = jnp.sum(grad_soft * softmax_out, axis=-1, keepdims=True)
    grad_scores = (softmax_out * (grad_soft - row_inner) * score_scale).astype(jnp.bfloat16)
    grad_query = jnp.einsum(
        "bgrtu,bugh->btgrh", grad_scores, key_heads, preferred_element_type=jnp.float32
    ).astype(jnp.bfloat16)
    grad_key = jnp.einsum(
        "bgrtu,btgrh->bugh", grad_scores, query_heads, preferred_element_type=jnp.float32
    ).astype(jnp.bfloat16)
    grad_value = jnp.einsum(
        "bgrtu,btgrh->bugh", softmax_low, grad_context, preferred_element_type=jnp.float32
    ).astype(jnp.bfloat16)
    return (grad_query, grad_key, grad_value)


def on_device(tokens, grad_out, counts, gain, wq, wk, wv, wo):
    groups = lax.axis_size("tensor")
    replica = lax.axis_index("dp")
    own_count = counts[replica]
    gain_all, wq_all, wk_all, wv_all, wo_all = (
        lax.all_gather(gain, "dp", axis=0, tiled=True),
        lax.all_gather(wq, "dp", axis=0, tiled=True),
        lax.all_gather(wk, "dp", axis=0, tiled=True),
        lax.all_gather(wv, "dp", axis=0, tiled=True),
        lax.all_gather(wo, "dp", axis=1, tiled=True),
    )
    live_mask = (jnp.arange(tokens.shape[0]) < own_count).astype(jnp.bfloat16)[:, None, None]
    block_grad = grad_out * live_mask
    wide_in, upstream = (
        lax.all_gather(tokens, "tensor", axis=2, tiled=True),
        lax.all_gather(block_grad, "tensor", axis=2, tiled=True),
    )
    blocks, length, full_width = wide_in.shape
    repeat = HEADS // KV
    kv_local = wk_all.shape[1] // HD
    wide_float = wide_in.astype(jnp.float32)
    inverse_rms = lax.rsqrt(jnp.mean(wide_float * wide_float, axis=-1, keepdims=True) + epsilon)
    unit_rows = wide_float * inverse_rms
    gain_float = gain_all.astype(jnp.float32)
    normed = (unit_rows * gain_float).astype(jnp.bfloat16)
    queries = jnp.einsum("btd,dk->btk", normed, wq_all, preferred_element_type=jnp.float32).astype(
        jnp.bfloat16
    )
    key_rows = jnp.einsum("btd,dk->btk", normed, wk_all, preferred_element_type=jnp.float32).astype(
        jnp.bfloat16
    )
    values = jnp.einsum("btd,dk->btk", normed, wv_all, preferred_element_type=jnp.float32).astype(
        jnp.bfloat16
    )
    query_heads = queries.reshape(blocks, length, kv_local, repeat, HD)
    key_heads = key_rows.reshape(blocks, length, kv_local, HD)
    value_heads = values.reshape(blocks, length, kv_local, HD)
    softmax_out, softmax_low, context = attention_forward(query_heads, key_heads, value_heads)
    context_flat = context.reshape(blocks, length, kv_local * repeat * HD)
    partial_value = jnp.einsum(
        "btk,kd->btd", context_flat, wo_all, preferred_element_type=jnp.float32
    )
    attn_sum = lax.psum_scatter(
        partial_value.astype(jnp.bfloat16), "tensor", scatter_dimension=2, tiled=True
    ).astype(jnp.float32)
    mixed_block = ((tokens.astype(jnp.float32) + attn_sum) * live_mask.astype(jnp.float32)).astype(
        jnp.bfloat16
    )
    grad_context = jnp.einsum(
        "btd,kd->btk", upstream, wo_all, preferred_element_type=jnp.float32
    ).astype(jnp.bfloat16)
    grad_output_proj = jnp.einsum(
        "btk,btd->kd", context_flat, upstream, preferred_element_type=jnp.float32
    )
    grad_query, grad_key, grad_value = attention_backward(
        grad_context.reshape(blocks, length, kv_local, repeat, HD),
        query_heads,
        key_heads,
        value_heads,
        softmax_out,
        softmax_low,
    )
    grad_query = grad_query.reshape(blocks, length, -1)
    grad_key = grad_key.reshape(blocks, length, -1)
    grad_value = grad_value.reshape(blocks, length, -1)
    normed_terms = jnp.einsum("btk,dk->btd", grad_query, wq_all, preferred_element_type=jnp.float32)
    normed_terms = normed_terms + jnp.einsum(
        "btk,dk->btd", grad_key, wk_all, preferred_element_type=jnp.float32
    )
    normed_terms = normed_terms + jnp.einsum(
        "btk,dk->btd", grad_value, wv_all, preferred_element_type=jnp.float32
    )
    grad_query_proj = jnp.einsum(
        "btd,btk->dk", normed, grad_query, preferred_element_type=jnp.float32
    )
    grad_key_proj = jnp.einsum("btd,btk->dk", normed, grad_key, preferred_element_type=jnp.float32)
    grad_value_proj = jnp.einsum(
        "btd,btk->dk", normed, grad_value, preferred_element_type=jnp.float32
    )
    shard_width = full_width // groups
    shard_start = lax.axis_index("tensor") * shard_width
    grad_normed = lax.psum(normed_terms.astype(jnp.bfloat16), "tensor").astype(jnp.float32)
    scaled = grad_normed * gain_float
    row_mean = jnp.mean(scaled * unit_rows, axis=-1, keepdims=True)
    full_grad = inverse_rms * (scaled - unit_rows * row_mean)
    own_grad = lax.dynamic_slice_in_dim(full_grad, shard_start, shard_width, 2)
    gain_term = jnp.sum(grad_normed * unit_rows, axis=(0, 1))
    grad_block = (block_grad.astype(jnp.float32) + own_grad).astype(jnp.bfloat16)
    grad_gain, grad_wq, grad_wk, grad_wv, grad_wo = (
        lax.psum_scatter(
            gain_term.astype(jnp.bfloat16), "dp", scatter_dimension=0, tiled=True
        ).astype(jnp.float32),
        lax.psum_scatter(
            grad_query_proj.astype(jnp.bfloat16), "dp", scatter_dimension=0, tiled=True
        ).astype(jnp.float32),
        lax.psum_scatter(
            grad_key_proj.astype(jnp.bfloat16), "dp", scatter_dimension=0, tiled=True
        ).astype(jnp.float32),
        lax.psum_scatter(
            grad_value_proj.astype(jnp.bfloat16), "dp", scatter_dimension=0, tiled=True
        ).astype(jnp.float32),
        lax.psum_scatter(
            grad_output_proj.astype(jnp.bfloat16), "dp", scatter_dimension=1, tiled=True
        ).astype(jnp.float32),
    )
    return (mixed_block, grad_block, grad_gain, grad_wq, grad_wk, grad_wv, grad_wo)


def solution(mesh):
    return jax.shard_map(
        on_device,
        mesh=mesh,
        in_specs=(
            P("dp", None, "tensor"),
            P("dp", None, "tensor"),
            P(),
            P("dp"),
            P("dp", "tensor"),
            P("dp", "tensor"),
            P("dp", "tensor"),
            P("tensor", "dp"),
        ),
        out_specs=(
            P("dp", None, "tensor"),
            P("dp", None, "tensor"),
            P("dp"),
            P("dp", "tensor"),
            P("dp", "tensor"),
            P("dp", "tensor"),
            P("tensor", "dp"),
        ),
        check_vma=False,
    )
```

profile of v0, /device:TPU:4, one launch (start us, length us, event | category | flops | bytes accessed | tf_op | source)
XLA Modules:
  0.0 1012.3 jit_solution(5236117087255175086)
XLA Ops:
  7.2 0.7 all-gather.8.cloned.1.call-update
  7.9 0.7 all-gather.12.cloned.1.call-update
  8.7 0.7 all-gather.14.cloned.1.call-update
  9.4 1.2 dynamic_slice.6
  10.7 0.6 compare_convert_fusion
  11.3 0.5 copy-done.13
  11.8 1.8 broadcast_multiply_fusion
  13.8 0.5 all-gather.16.cloned.1.call-update
  14.3 0.5 all-gather.10.cloned.1.call-update
  14.9 40.9 %all-gather = bf16[32,1,128]{2,1,0:T(2,128)(2,1)S(1)} all-gather(bf16[1,1,128]{2,1,0:T(2,128)(2,1)} %bitcast.161), channel_id=1, replica_groups=mesh['dp'=32,'tensor'=8] {'dp'}, dimensions={0}, use_global_device_ids=true | all-gather | bytes 8448 | tf_op jit(solution)/shard_map/all_gather | solution.py:58
  55.9 31.1 %all-gather.8.cloned.1.call-done = bf16[2,192,4096]{2,1,0:T(8,128)(2,1)} async-done(((bf16[2,192,512]{2,1,0:T(8,128)(2,1)}), bf16[2,192,4096]{2,1,0:T(8,128)(2,1)}) %all-gather.8.cloned.1.call-update) | async-done | bytes 3145744 | tf_op jit(solution)/shard_map/all_gather | solution.py:67
  87.0 2.7 fusion
  89.7 49.9 %all-gather.12.cloned.1.call-done = bf16[4096,128]{1,0:T(8,128)(2,1)} async-done(((bf16[128,128]{1,0:T(8,128)(2,1)}), bf16[4096,128]{1,0:T(8,128)(2,1)}) %all-gather.12.cloned.1.call-update) | async-done | bytes 1048592 | tf_op jit(solution)/shard_map/all_gather | solution.py:60
  139.7 2.3 fusion.34
  141.9 59.2 %all-gather.14.cloned.1.call-done = bf16[4096,512]{1,0:T(8,128)(2,1)} async-done(((bf16[128,512]{1,0:T(8,128)(2,1)}), bf16[4096,512]{1,0:T(8,128)(2,1)}) %all-gather.14.cloned.1.call-update) | async-done | bytes 4194320 | tf_op jit(solution)/shard_map/all_gather | solution.py:59
  201.1 4.0 fusion.28
  205.2 0.7 copy-done.10
  205.9 0.4 fusion.62
  206.6 69.3 %all-gather.18.cloned.1.call-done = bf16[2,192,4096]{2,1,0:T(8,128)(2,1)} async-done(((bf16[2,192,512]{2,1,0:T(8,128)(2,1)}), bf16[2,192,4096]{2,1,0:T(8,128)(2,1)}) %all-gather.18.cloned.1.call-update) | async-done | bytes 3145744 | tf_op jit(solution)/shard_map/all_gather | solution.py:68
  275.9 65.8 %all-gather.16.cloned.1.call-done = bf16[512,4096]{1,0:T(8,128)(2,1)} async-done(((bf16[512,128]{1,0:T(8,128)(2,1)}), bf16[512,4096]{1,0:T(8,128)(2,1)}) %all-gather.16.cloned.1.call-update) | async-done | bytes 4194320 | tf_op jit(solution)/shard_map/all_gather | solution.py:62
  341.7 5.0 fusion.25
  346.7 0.4 fusion.35
  347.1 1.5 copy-done.1
  348.5 2.3 fusion.3
  350.9 41.3 %all-gather.10.cloned.1.call-done = bf16[4096,128]{1,0:T(8,128)(2,1)} async-done(((bf16[128,128]{1,0:T(8,128)(2,1)}), bf16[4096,128]{1,0:T(8,128)(2,1)}) %all-gather.10.cloned.1.call-update) | async-done | bytes 1048592 | tf_op jit(solution)/shard_map/all_gather | solution.py:61
  392.2 3.2 fusion.33
  395.4 0.5 fusion.11
  395.9 0.5 fusion.42
  396.4 0.5 copy-done.11
  396.9 0.4 fusion.36
  397.3 0.6 copy-done.2
  397.9 2.3 fusion.2
  400.5 0.5 fusion.24
  401.0 0.3 copy.34
  401.5 2.4 fusion.37
  404.0 1.9 fusion.7
  405.9 2.8 add_convert_fusion
  408.8 0.5 fusion.23
  409.8 6.4 bitcast_convert_fusion
  416.2 6.5 copy.43
  422.7 1.8 copy-done.3
  424.6 5.2 bitcast_convert_fusion.1
  430.0 0.7 copy-done.8
  430.8 5.7 convolution_convert_fusion
  436.5 0.6 copy-done.15
  437.1 0.6 dynamic-slice
  438.4 1.2 fusion.59
  439.5 43.9 %reduce-scatter.14.cloned.1.call-done = bf16[128,128]{1,0:T(8,128)(2,1)} async-done(((bf16[4096,128]{1,0:T(8,128)(2,1)}), bf16[128,128]{1,0:T(8,128)(2,1)}) %reduce-scatter.14.cloned.1.call-update) | async-done | bytes 32784 | tf_op jit(solution)/shard_map/reduce_scatter | solution.py:151
  483.5 1.4 convert_element_type.173
  484.8 89.4 %reduce-scatter.12.cloned.1.call-done = bf16[128,128]{1,0:T(8,128)(2,1)} async-done(((bf16[4096,128]{1,0:T(8,128)(2,1)}), bf16[128,128]{1,0:T(8,128)(2,1)}) %reduce-scatter.12.cloned.1.call-update) | async-done | bytes 32784 | tf_op jit(solution)/shard_map/reduce_scatter | solution.py:148
  574.3 1.4 convert_element_type.171
  575.7 148.6 %all-reduce.3.cloned.1.call-done = bf16[2,192,4096]{2,1,0:T(8,128)(2,1)} async-done(((bf16[2,192,4096]{2,1,0:T(8,128)(2,1)}), bf16[2,192,4096]{2,1,0:T(8,128)(2,1)}) %all-reduce.3.cloned.1.call-update) | async-done | bytes 3145744 | tf_op jit(solution)/shard_map/psum | solution.py:134
  724.3 8.1 fusion.1
  732.4 67.0 %all-reduce = bf16[4096]{0:T(1024)(128)(2,1)S(1)} all-reduce(bf16[4096]{0:T(1024)(128)(2,1)} %get-tuple-element.7), channel_id=3, replica_groups=mesh['dp'=32,'tensor'=8] {'dp'}, use_global_device_ids=true, to_apply=%region_8.9.clone | all-reduce | flops 4096 | bytes 16384
  799.5 0.6 dynamic-slice_convert_fusion
  800.1 0.7 broadcast_multiply_fusion.1
  800.7 2.4 fusion.45
  803.2 23.6 %reduce-scatter.16.cloned.1.call-done = bf16[128,512]{1,0:T(8,128)(2,1)} async-done(((bf16[4096,512]{1,0:T(8,128)(2,1)}), bf16[128,512]{1,0:T(8,128)(2,1)}) %reduce-scatter.16.cloned.1.call-update) | async-done | bytes 131088
  826.7 1.0 copy.44
  827.7 0.7 convert_element_type.175
  828.5 99.3 %reduce-scatter.10.cloned.1.call-done = bf16[128,512]{1,0:T(8,128)(2,1)} async-done(((bf16[4096,512]{1,0:T(8,128)(2,1)}), bf16[128,512]{1,0:T(8,128)(2,1)}) %reduce-scatter.10.cloned.1.call-update) | async-done | bytes 131088 | tf_op jit(solution)/shard_map/reduce_scatter | solution.py:145
  927.7 1.6 convert_element_type.169
  929.4 74.2 %reduce-scatter.8.cloned.1.call-done = bf16[2,192,512]{2,1,0:T(8,128)(2,1)} async-done(((bf16[2,192,4096]{2,1,0:T(8,128)(2,1)}), bf16[2,192,512]{2,1,0:T(8,128)(2,1)}) %reduce-scatter.8.cloned.1.call-update) | async-done | bytes 393232 | tf_op jit(solution)/shard_map/reduce_scatter | solution.py:95
  1003.6 1.9 multiply_convert_fusion.1
  (50 shorter events, 2.1 us)
Async XLA Ops:
  7.2 79.8 %all-gather.8.cloned.1.call-start = ((), (), s32[]{:S(2)}) async-start(), calls=%async_computation.5 | async-start | bytes 3538944 | tf_op jit(solution)/shard_map/all_gather | solution.py:67
  7.9 131.8 %all-gather.12.cloned.1.call-start = ((), (), s32[]{:S(2)}) async-start(), calls=%async_computation.7 | async-start | bytes 1081344 | tf_op jit(solution)/shard_map/all_gather | solution.py:60
  8.6 192.5 %all-gather.14.cloned.1.call-start = ((), (), s32[]{:S(2)}) async-start(), calls=%async_computation.8 | async-start | bytes 4325376 | tf_op jit(solution)/shard_map/all_gather | solution.py:59
  9.4 266.5 %all-gather.18.cloned.1.call-start = ((), (), s32[]{:S(2)}) async-start(), calls=%async_computation.11 | async-start | bytes 3538944 | tf_op jit(solution)/shard_map/all_gather | solution.py:68
  11.3 0.5 copy-start.13
  13.7 328.0 %all-gather.16.cloned.1.call-start = ((), (), s32[]{:S(2)}) async-start(), calls=%async_computation.9 | async-start | bytes 4325376 | tf_op jit(solution)/shard_map/all_gather | solution.py:62
  14.3 377.9 %all-gather.10.cloned.1.call-start = ((), (), s32[]{:S(2)}) async-start(), calls=%async_computation.6 | async-start | bytes 1081344 | tf_op jit(solution)/shard_map/all_gather | solution.py:61
  14.9 468.6 %reduce-scatter.14.cloned.1.call-start = ((), (), s32[]{:S(2)}) async-start(), calls=%async_computation.15 | async-start | bytes 1081344 | tf_op jit(solution)/shard_map/reduce_scatter | solution.py:151
  87.0 52.7 %copy-start = (bf16[2,192,4096]{2,1,0:T(8,128)(2,1)S(1)}, bf16[2,192,4096]{2,1,0:T(8,128)(2,1)}, u32[]{:S(2)}) copy-start(bf16[2,192,4096]{2,1,0:T(8,128)(2,1)} %all-gather.8.cloned.1.call-done) | copy-start | bytes 9437188
  89.7 307.5 %copy-start.12 = (f32[2,192]{1,0:T(2,128)}, f32[2,192]{1,0:T(2,128)S(1)}, u32[]{:S(2)}) copy-start(f32[2,192]{1,0:T(2,128)S(1)} %add_rsqrt_fusion) | copy-start | bytes 4612
  205.1 0.7 copy-start.10
  346.7 1.9 copy-start.1
  350.9 223.4 %reduce-scatter.12.cloned.1.call-start = ((), (), s32[]{:S(2)}) async-start(), calls=%async_computation.14 | async-start | bytes 1081344 | tf_op jit(solution)/shard_map/reduce_scatter | solution.py:148
  395.9 1.0 copy-start.11
  395.9 2.0 copy-start.2
  400.3 324.0 %all-reduce.3.cloned.1.call-start = ((), (), s32[]{:S(2)}) async-start(), calls=%async_computation.12 | async-start | bytes 6291456 | tf_op jit(solution)/shard_map/psum | solution.py:134
  401.5 2.5 copy-start.4
  404.0 1.9 copy-start.9
  408.7 418.0 %reduce-scatter.16.cloned.1.call-start = ((), (), s32[]{:S(2)}) async-start(), calls=%async_computation.16 | async-start | bytes 4325376
  409.8 6.4 copy-start.7
  422.7 1.9 copy-start.3
  422.7 505.1 %reduce-scatter.10.cloned.1.call-start = ((), (), s32[]{:S(2)}) async-start(), calls=%async_computation.13 | async-start | bytes 4325376 | tf_op jit(solution)/shard_map/reduce_scatter | solution.py:145
  429.8 1.0 copy-start.8
  429.8 573.8 %reduce-scatter.8.cloned.1.call-start = ((), (), s32[]{:S(2)}) async-start(), calls=%async_computation.10 | async-start | bytes 3538944 | tf_op jit(solution)/shard_map/reduce_scatter | solution.py:95
  436.5 0.7 copy-start.15
  575.7 225.1 %copy-start.6 = (bf16[2,192,512]{2,1,0:T(8,128)(2,1)S(1)}, bf16[2,192,512]{2,1,0:T(8,128)(2,1)}, u32[]{:S(2)}) copy-start(bf16[2,192,512]{2,1,0:T(8,128)(2,1)} %param.9) | copy-start | bytes 1179652
  732.4 271.2 %copy-start.5 = (bf16[2,192,512]{2,1,0:T(8,128)(2,1)S(1)}, bf16[2,192,512]{2,1,0:T(8,128)(2,1)}, u32[]{:S(2)}) copy-start(bf16[2,192,512]{2,1,0:T(8,128)(2,1)} %param.8) | copy-start | bytes 1179652
  732.4 271.2 %copy-start.14 = (f32[2]{0:T(128)S(1)}, f32[2]{0:T(128)}, u32[]{:S(2)}) copy-start(f32[2]{0:T(128)} %fusion.59) | copy-start | bytes 28
Sparse Core Ops, SparseCore 0:
  9.8 77.1 all-gather.7
  89.5 50.1 all-gather.11
  142.2 58.8 all-gather.13
  203.3 72.4 all-gather.17
  278.2 63.4 all-gather.15
  344.1 48.0 all-gather.9
  396.0 87.4 reduce-scatter.13
  487.2 87.0 reduce-scatter.11
  577.0 147.3 all-reduce.2
  728.1 98.5 reduce-scatter.15
  830.7 97.0 reduce-scatter.9
  930.2 73.3 reduce-scatter.7
where the time goes:
time: 1010 us
  waiting for transfers between devices  799 us (79%)
  blocking collectives  108 us (11%)
  matrix products  46.1 us (5%)
  other arithmetic  26 us (3%)
  local copies, waits for them, and re-layouts  17.4 us (2%)
  between operations  15.1 us (1%)
    psum x1, waiting for transfers between devices, on_device(): lax.psum(normed_terms.astype(jnp.bfloat16), 'tensor').astype(jnp.float32)  149 us
    reduce_scatter x1, waiting for transfers between devices, on_device(): lax.psum_scatter(grad_query_proj.astype(jnp.bfloat16), 'dp', scatter_dime...  99.3 us
    reduce_scatter x1, waiting for transfers between devices, on_device(): lax.psum_scatter(grad_key_proj.astype(jnp.bfloat16), 'dp', scatter_dimens...  89.4 us
    reduce_scatter x1, waiting for transfers between devices, on_device(): lax.psum_scatter(partial_value.astype(jnp.bfloat16), 'tensor', scatter_di...  74.2 us
    all_gather x1, waiting for transfers between devices, on_device(): lax.all_gather(block_grad, 'tensor', axis=2, tiled=True)  69.3 us
    unnamed x1, blocking collectives  67 us
    all_gather x1, waiting for transfers between devices, on_device(): lax.all_gather(wo, 'dp', axis=1, tiled=True)  65.8 us
    all_gather x1, waiting for transfers between devices, on_device(): lax.all_gather(wq, 'dp', axis=0, tiled=True)  59.2 us
  transfers between devices with their start and end apart: 12, of which 12 were waited for; matrix products, arithmetic and copies ran while one was open for 8% of the time, Pallas kernels for 0%

commit v1 on v0

--- a/solution.py
+++ b/solution.py
@@ -52,29 +52,49 @@
 
 def on_device(tokens, grad_out, counts, gain, wq, wk, wv, wo):
     groups = lax.axis_size("tensor")
+    dp_size = lax.axis_size("dp")
     replica = lax.axis_index("dp")
     own_count = counts[replica]
-    gain_all, wq_all, wk_all, wv_all, wo_all = (
-        lax.all_gather(gain, "dp", axis=0, tiled=True),
-        lax.all_gather(wq, "dp", axis=0, tiled=True),
-        lax.all_gather(wk, "dp", axis=0, tiled=True),
-        lax.all_gather(wv, "dp", axis=0, tiled=True),
-        lax.all_gather(wo, "dp", axis=1, tiled=True),
-    )
-    live_mask = (jnp.arange(tokens.shape[0]) < own_count).astype(jnp.bfloat16)[:, None, None]
+    blocks, length, shard_width = tokens.shape
+    full_width = shard_width * groups
+    d_local = gain.shape[0]
+    q_cols = wq.shape[1]
+    k_cols = wk.shape[1]
+    o_rows = wo.shape[0]
+    lane = wo.shape[1]
+    pack = jnp.concatenate(
+        [
+            jnp.pad(gain.reshape(1, d_local), ((0, 7), (0, 0))),
+            wq.reshape(d_local * q_cols // lane, lane),
+            wk.reshape(d_local * k_cols // lane, lane),
+            wv.reshape(d_local * k_cols // lane, lane),
+            wo,
+        ],
+        axis=0,
+    )
+    packed = lax.all_gather(pack, "dp", axis=0, tiled=False)
+    r0 = 8
+    r1 = r0 + d_local * q_cols // lane
+    r2 = r1 + d_local * k_cols // lane
+    r3 = r2 + d_local * k_cols // lane
+    r4 = r3 + o_rows
+    gain_all = packed[:, 0, :].reshape(full_width)
+    wq_all = packed[:, r0:r1, :].reshape(dp_size * d_local, q_cols)
+    wk_all = packed[:, r1:r2, :].reshape(dp_size * d_local, k_cols)
+    wv_all = packed[:, r2:r3, :].reshape(dp_size * d_local, k_cols)
+    wo_blk = packed[:, r3:r4, :]
+    live_mask = (jnp.arange(blocks) < own_count).astype(jnp.bfloat16)[:, None, None]
     block_grad = grad_out * live_mask
-    wide_in, upstream = (
-        lax.all_gather(tokens, "tensor", axis=2, tiled=True),
-        lax.all_gather(block_grad, "tensor", axis=2, tiled=True),
-    )
-    blocks, length, full_width = wide_in.shape
+    both = lax.all_gather(jnp.stack([tokens, block_grad]), "tensor", axis=3, tiled=True)
+    wide_in, upstream = both[0], both[1]
     repeat = HEADS // KV
     kv_local = wk_all.shape[1] // HD
     wide_float = wide_in.astype(jnp.float32)
     inverse_rms = lax.rsqrt(jnp.mean(wide_float * wide_float, axis=-1, keepdims=True) + epsilon)
     unit_rows = wide_float * inverse_rms
     gain_float = gain_all.astype(jnp.float32)
-    normed = (unit_rows * gain_float).astype(jnp.bfloat16)
+    normed_float = unit_rows * gain_float
+    normed = normed_float.astype(jnp.bfloat16)
     queries = jnp.einsum("btd,dk->btk", normed, wq_all, preferred_element_type=jnp.float32).astype(
         jnp.bfloat16
     )
@@ -90,19 +110,14 @@
     softmax_out, softmax_low, context = attention_forward(query_heads, key_heads, value_heads)
     context_flat = context.reshape(blocks, length, kv_local * repeat * HD)
     partial_value = jnp.einsum(
-        "btk,kd->btd", context_flat, wo_all, preferred_element_type=jnp.float32
-    )
-    attn_sum = lax.psum_scatter(
-        partial_value.astype(jnp.bfloat16), "tensor", scatter_dimension=2, tiled=True
-    ).astype(jnp.float32)
-    mixed_block = ((tokens.astype(jnp.float32) + attn_sum) * live_mask.astype(jnp.float32)).astype(
-        jnp.bfloat16
-    )
+        "btk,jkl->btjl", context_flat, wo_blk, preferred_element_type=jnp.float32
+    ).reshape(blocks, length, full_width)
+    upstream_blk = upstream.reshape(blocks, length, dp_size, lane)
     grad_context = jnp.einsum(
-        "btd,kd->btk", upstream, wo_all, preferred_element_type=jnp.float32
+        "btjl,jkl->btk", upstream_blk, wo_blk, preferred_element_type=jnp.float32
     ).astype(jnp.bfloat16)
     grad_output_proj = jnp.einsum(
-        "btk,btd->kd", context_flat, upstream, preferred_element_type=jnp.float32
+        "btk,btjl->jkl", context_flat, upstream_blk, preferred_element_type=jnp.float32
     )
     grad_query, grad_key, grad_value = attention_backward(
         grad_context.reshape(blocks, length, kv_local, repeat, HD),
@@ -129,32 +144,63 @@
     grad_value_proj = jnp.einsum(
         "btd,btk->dk", normed, grad_value, preferred_element_type=jnp.float32
     )
-    shard_width = full_width // groups
+    term_low = normed_terms.astype(jnp.bfloat16)
+    term_float = term_low.astype(jnp.float32)
+    rows = blocks * length
+    row_dot = jnp.sum(term_float * normed_float, axis=-1).reshape(rows)
+    gain_part = jnp.sum(term_float * unit_rows, axis=(0, 1))
+    extra_rows = 1 + full_width // shard_width
+    extra = jnp.concatenate(
+        [
+            jnp.pad(row_dot, (0, shard_width - rows)).reshape(1, shard_width),
+            gain_part.reshape(full_width // shard_width, shard_width),
+        ],
+        axis=0,
+    )
+    extra_pad = (-extra_rows) % 8
+    extra = jnp.pad(extra, ((0, extra_pad), (0, 0))).astype(jnp.bfloat16)
+
+    def by_chunk(x):
+        return x.reshape(rows, groups, shard_width).transpose(1, 0, 2)
+
+    payload = jnp.concatenate(
+        [
+            by_chunk(partial_value.astype(jnp.bfloat16)),
+            by_chunk(term_low),
+            jnp.broadcast_to(extra[None], (groups,) + extra.shape),
+        ],
+        axis=1,
+    )
+    reduced = lax.psum_scatter(payload, "tensor", scatter_dimension=0, tiled=True)[0]
+    reduced = reduced.astype(jnp.float32)
+    attn_sum = reduced[:rows].reshape(blocks, length, shard_width)
+    grad_normed = reduced[rows : 2 * rows].reshape(blocks, length, shard_width)
+    row_mean = (reduced[2 * rows, :rows] / full_width).reshape(blocks, length, 1)
+    gain_term = reduced[2 * rows + 1 : 2 * rows + extra_rows].reshape(full_width)
+    mixed_block = ((tokens.astype(jnp.float32) + attn_sum) * live_mask.astype(jnp.float32)).astype(
+        jnp.bfloat16
+    )
     shard_start = lax.axis_index("tensor") * shard_width
-    grad_normed = lax.psum(normed_terms.astype(jnp.bfloat16), "tensor").astype(jnp.float32)
-    scaled = grad_normed * gain_float
-    row_mean = jnp.mean(scaled * unit_rows, axis=-1, keepdims=True)
-    full_grad = inverse_rms * (scaled - unit_rows * row_mean)
-    own_grad = lax.dynamic_slice_in_dim(full_grad, shard_start, shard_width, 2)
-    gain_term = jnp.sum(grad_normed * unit_rows, axis=(0, 1))
+    own_unit = lax.dynamic_slice_in_dim(unit_rows, shard_start, shard_width, 2)
+    own_gain = lax.dynamic_slice_in_dim(gain_float, shard_start, shard_width, 0)
+    own_grad = inverse_rms * (grad_normed * own_gain - own_unit * row_mean)
     grad_block = (block_grad.astype(jnp.float32) + own_grad).astype(jnp.bfloat16)
-    grad_gain, grad_wq, grad_wk, grad_wv, grad_wo = (
-        lax.psum_scatter(
-            gain_term.astype(jnp.bfloat16), "dp", scatter_dimension=0, tiled=True
-        ).astype(jnp.float32),
-        lax.psum_scatter(
-            grad_query_proj.astype(jnp.bfloat16), "dp", scatter_dimension=0, tiled=True
-        ).astype(jnp.float32),
-        lax.psum_scatter(
-            grad_key_proj.astype(jnp.bfloat16), "dp", scatter_dimension=0, tiled=True
-        ).astype(jnp.float32),
-        lax.psum_scatter(
-            grad_value_proj.astype(jnp.bfloat16), "dp", scatter_dimension=0, tiled=True
-        ).astype(jnp.float32),
-        lax.psum_scatter(
-            grad_output_proj.astype(jnp.bfloat16), "dp", scatter_dimension=1, tiled=True
-        ).astype(jnp.float32),
-    )
+    gpack = jnp.concatenate(
+        [
+            jnp.pad(gain_term.reshape(dp_size, 1, d_local), ((0, 0), (0, 7), (0, 0))),
+            grad_query_proj.reshape(dp_size, d_local * q_cols // lane, lane),
+            grad_key_proj.reshape(dp_size, d_local * k_cols // lane, lane),
+            grad_value_proj.reshape(dp_size, d_local * k_cols // lane, lane),
+            grad_output_proj,
+        ],
+        axis=1,
+    ).astype(jnp.bfloat16)
+    greduced = lax.psum_scatter(gpack, "dp", scatter_dimension=0, tiled=True)[0].astype(jnp.float32)
+    grad_gain = greduced[0]
+    grad_wq = greduced[r0:r1].reshape(d_local, q_cols)
+    grad_wk = greduced[r1:r2].reshape(d_local, k_cols)
+    grad_wv = greduced[r2:r3].reshape(d_local, k_cols)
+    grad_wo = greduced[r3:r4]
     return (mixed_block, grad_block, grad_gain, grad_wq, grad_wk, grad_wv, grad_wo)
 
 

time: 1010 us -> 637 us (0.63); the launches traced: 1010 us -> 626 us
  waiting for transfers between devices: 799 us -> 449 us
  blocking collectives: 108 us -> 0 us
  local copies, waits for them, and re-layouts: 17.4 us -> 95.4 us
    psum x1 -> x0, waiting for transfers between devices: 149 us -> none  [on_device(): lax.psum(normed_terms.astype(jnp.bfloat16), 'tensor').astype(jnp.float32)]
    all_gather x6 -> x2, waiting for transfers between devices: 317 us -> 220 us  [the longest x1 134 us: on_device(): lax.all_gather(jnp.stack([tokens, block_grad]), 'tensor', axis=3, tiled=T...]
    reduce_scatter x4 -> x2, waiting for transfers between devices: 307 us -> 229 us  [the longest x1 133 us: on_device(): lax.psum_scatter(gpack, 'dp', scatter_dimension=0, tiled=True)[0]]
    unnamed x1 -> x0, blocking collectives: 67 us -> none
    all_gather x1 -> x0, blocking collectives: 40.9 us -> none  [on_device(): lax.all_gather(gain, 'dp', axis=0, tiled=True)]
    unnamed x13 -> x4, waiting for transfers between devices: 26.8 us -> 0.07 us
    reshape x0 -> x8, local copies, waits for them, and re-layouts: none -> 26.1 us  [the longest x2 14.6 us: on_device(): grad_query_proj.reshape(dp_size, d_local * q_cols // lane, lane)]
    concatenate x0 -> x2, local copies, waits for them, and re-layouts: none -> 19.6 us  [the longest x1 19.6 us: on_device(): jnp.concatenate([jnp.pad(gain_term.reshape(dp_size, 1, d_local), ((0, 0),...]
  transfers between devices with their start and end apart: 12 -> 4, of which waited for: 12 -> 4; matrix products, arithmetic and copies ran while one was open for 8% -> 7% of each run, Pallas kernels for 0% -> 0%
where the time goes in v1:
time: 637 us; the launch traced here: 626 us
  waiting for transfers between devices  449 us (70%)
  local copies, waits for them, and re-layouts  95.4 us (15%)
  matrix products  43.1 us (7%)
  other arithmetic  23.3 us (4%)
  between operations  14.8 us (2%)
    all_gather x1, waiting for transfers between devices, on_device(): lax.all_gather(jnp.stack([tokens, block_grad]), 'tensor', axis=3, tiled=T...  134 us
    reduce_scatter x1, waiting for transfers between devices, on_device(): lax.psum_scatter(gpack, 'dp', scatter_dimension=0, tiled=True)[0]  133 us
    reduce_scatter x1, waiting for transfers between devices, on_device(): lax.psum_scatter(payload, 'tensor', scatter_dimension=0, tiled=True)[0]  96.2 us
    all_gather x1, waiting for transfers between devices, on_device(): packed = lax.all_gather(pack, 'dp', axis=0, tiled=False)  86.4 us
    concatenate x1, local copies, waits for them, and re-layouts, on_device(): jnp.concatenate([jnp.pad(gain_term.reshape(dp_size, 1, d_local), ((0, 0),...  19.6 us
    reshape x2, local copies, waits for them, and re-layouts, on_device(): grad_query_proj.reshape(dp_size, d_local * q_cols // lane, lane)  14.6 us
    unnamed x84, local copies, waits for them, and re-layouts  14.5 us
    dot_general x2, local copies, waits for them, and re-layouts, on_device(): jnp.einsum('btk,jkl->btjl', context_flat, wo_blk, preferred_element_type=...  13.3 us
  transfers between devices with their start and end apart: 4, of which 4 were waited for; matrix products, arithmetic and copies ran while one was open for 7% of the time, Pallas kernels for 0%

profile of v1, /device:TPU:4, one launch (start us, length us, event | category | flops | bytes accessed | tf_op | source)
XLA Modules:
  0.0 626.0 jit_solution(15260371974625475414)
XLA Ops:
  7.3 1.3 dynamic_slice.9
  8.6 0.6 compare_convert_fusion
  9.2 0.6 copy-done.30
  9.8 1.1 multiply_bitcast_fusion
  10.9 2.0 pad_maximum_fusion.1
  13.2 0.7 copy-done.18
  14.0 134.0 %all-gather.4.cloned.1.call-done = bf16[2,2,192,4096]{3,2,1,0:T(8,128)(2,1)} async-done(((bf16[2,2,192,512]{3,2,1,0:T(8,128)(2,1)}), bf16[2,2,192,4096]{3,2,1,0:T(8,128)(2,1)}) %all-gather.4.cloned.1.call-update) | async-done | bytes 6291472 | tf_op jit(solution)/shard_map/all_gather | solution.py:88
  148.0 1.9 slice-done.4
  149.9 2.5 copy.68
  152.4 1.4 copy-done.1
  153.8 0.7 fusion.2
  154.5 86.4 %all-gather.6.cloned.1.call-done = bf16[41216,128]{1,0:T(8,128)(2,1)} async-done(((bf16[1288,128]{1,0:T(8,128)(2,1)}), bf16[41216,128]{1,0:T(8,128)(2,1)}) %all-gather.6.cloned.1.call-update) | async-done | bytes 10551312 | tf_op jit(solution)/shard_map/all_gather | solution.py:75
  241.0 0.8 slice_convert_fusion
  241.8 1.7 fusion.83
  243.6 6.6 %slice_bitcast_fusion = (bf16[32,128,512]{1,2,0:T(8,128)(2,1)}, bf16[32,512,128]{2,1,0:T(8,128)(2,1)}) fusion(bf16[32,1288,128]{2,1,0:T(8,128)(2,1)} %bitcast.235), kind=kLoop, calls=%fused_computation.21 | loop fusion | bytes 16777216 | tf_op jit(solution)/shard_map/btk,jkl->btjl/dot_general | solution.py:112
  250.1 4.2 fusion.44
  254.3 7.5 %reshape.219 = bf16[4096,512,1]{1,0,2:T(8,128)(2,1)} reshape(bf16[32,512,128]{2,1,0:T(8,128)(2,1)} %get-tuple-element.24) | data formatting | bytes 8388608 | tf_op jit(solution)/shard_map/reshape | solution.py:82
  261.9 3.1 fusion.52
  265.0 4.0 fusion.43
  269.7 1.1 fusion.50
  270.8 1.0 fusion.51
  271.9 0.5 fusion.41
  272.4 0.5 fusion.25
  273.7 0.5 fusion.42
  274.2 6.7 %copy.34 = bf16[32,128,512]{2,1,0:T(8,128)(2,1)} copy(bf16[32,128,512]{1,2,0:T(8,128)(2,1)} %get-tuple-element.23) | data formatting | bytes 8388608 | tf_op jit(solution)/shard_map/btk,jkl->btjl/dot_general | solution.py:112
  281.4 4.0 convolution_convert_fusion
  285.4 3.2 copy.67
  289.0 4.2 fusion.86
  293.3 1.0 fusion.70
  294.5 1.0 add_convert_fusion
  295.8 0.9 slice-done.3
  296.6 6.1 fusion.5
  302.7 1.3 reshape.207
  304.0 0.7 pad.20
  304.7 0.6 reshape.208
  305.3 1.3 reshape.209
  306.6 1.4 copy.69
  308.5 2.3 copy_bitcast_fusion
  310.8 6.2 pad_maximum_fusion
  317.1 0.9 reshape.232
  318.0 6.5 %bitcast_convert_fusion.1 = bf16[4096,512]{1,0:T(8,128)(2,1)} fusion(bf16[2,192,512]{2,1,0:T(8,128)(2,1)S(1)} %copy-done.14, f32[4096]{0:T(1024)S(1)} %bitcast.250, f32[2,192]{1,0:T(2,128)S(1)} %copy-done.27, bf16[2,2,192,4096]{3,2,1,0:T(8,128)(2,1)} %all-gather.4.cloned.1.call-done), kind=kOutput, calls=%fused_computation.1 | convolution fusion | flops 1619001344 | bytes 7751168 | tf_op jit(solution)/shard_map/btd,btk->dk/dot_general | solution.py:140
  324.5 7.9 %reshape.212 = bf16[32,512,128]{2,1,0:T(8,128)(2,1)} reshape(bf16[4096,512]{1,0:T(8,128)(2,1)} %bitcast_convert_fusion.1) | data formatting | bytes 8388608 | tf_op jit(solution)/shard_map/reshape | solution.py:191
  332.4 6.6 %copy.47 = bf16[32,512,128]{1,2,0:T(8,128)(2,1)} copy(bf16[32,512,128]{2,1,0:T(8,128)(2,1)} %reshape.212) | data formatting | bytes 8388608 | tf_op jit(solution)/shard_map/reshape | solution.py:191
  339.1 2.0 bitcast_convert_fusion.3
  341.1 2.3 copy.48
  343.4 4.1 bitcast_convert_fusion.2
  347.5 2.2 copy.49
  349.7 4.7 fusion.7
  354.4 96.2 %reduce-scatter.3.cloned.1.call-done = bf16[1,784,512]{2,1,0:T(8,128)(2,1)} async-done(((bf16[8,784,512]{2,1,0:T(8,128)(2,1)}), bf16[1,784,512]{2,1,0:T(8,128)(2,1)}) %reduce-scatter.3.cloned.1.call-update) | async-done | bytes 802832 | tf_op jit(solution)/shard_map/reduce_scatter | solution.py:174
  450.6 0.7 slice.92
  451.3 3.2 reshape_reshape.5
  454.5 1.5 pad.22
  456.0 19.6 %concatenate.17 = bf16[32,1288,128]{1,2,0:T(8,128)(2,1)} concatenate(bf16[32,8,128]{1,2,0:T(8,128)(2,1)S(1)} %pad.22, bf16[32,512,128]{1,2,0:T(8,128)(2,1)} %copy.47, bf16[32,128,128]{1,2,0:T(8,128)(2,1)S(1)} %copy-done.6, bf16[32,128,128]{1,2,0:T(8,128)(2,1)S(1)} %copy-done.7, bf16[32,512,128]{1,2,0:T(8,128)(2,1)} %fusion.7), dimensions={1} | concatenate | bytes 21102592 | tf_op jit(solution)/shard_map/concatenate | solution.py:188
  475.6 0.7 fusion.76
  477.3 0.9 multiply_convert_fusion.1
  478.2 2.1 add_convert_fusion.1
  480.4 132.5 %reduce-scatter.5.cloned.1.call-done = bf16[1,1288,128]{1,2,0:T(8,128)(2,1)} async-done(((bf16[32,1288,128]{1,2,0:T(8,128)(2,1)}), bf16[1,1288,128]{1,2,0:T(8,128)(2,1)}) %reduce-scatter.5.cloned.1.call-update) | async-done | bytes 329744 | tf_op jit(solution)/shard_map/reduce_scatter | solution.py:198
  612.9 1.0 convert_element_type.183
  613.9 0.6 slice_reduce_fusion
  614.8 1.0 slice.94
  616.0 0.7 reshape.213
  616.7 0.8 copy.53
  617.5 0.7 copy.52
  618.3 0.7 copy.51
  (107 shorter events, 5.3 us)
Async XLA Ops:
  7.2 5.8 copy-start.19
  7.2 5.9 copy-start.32
  7.2 5.9 copy-start.22
  7.2 5.9 copy-start.23
  7.2 5.9 copy-start.20
  7.2 140.8 %all-gather.4.cloned.1.call-start = ((), (), s32[]{:S(2)}) async-start(), calls=%async_computation.2 | async-start | bytes 7077888 | tf_op jit(solution)/shard_map/all_gather | solution.py:88
  9.2 0.6 copy-start.30
  12.9 228.1 %all-gather.6.cloned.1.call-start = ((), (), s32[]{:S(2)}) async-start(), calls=%async_computation.5 | async-start | bytes 10881024 | tf_op jit(solution)/shard_map/all_gather | solution.py:75
  13.2 0.7 copy-start.18
  13.9 436.6 %reduce-scatter.3.cloned.1.call-start = ((), (), s32[]{:S(2)}) async-start(), calls=%async_computation.3 | async-start | bytes 7225344 | tf_op jit(solution)/shard_map/reduce_scatter | solution.py:174
  148.0 1.9 slice-start.4
  149.9 3.9 copy-start.1
  154.5 116.3 %copy-start.25 = (f32[2,192]{1,0:T(2,128)}, f32[2,192]{1,0:T(2,128)S(1)}, u32[]{:S(2)}) copy-start(f32[2,192]{1,0:T(2,128)S(1)} %add_rsqrt_fusion) | copy-start | bytes 4612
  243.5 27.3 %copy-start.8 = (bf16[32,128,128]{2,1,0:T(8,128)(2,1)}, bf16[32,128,128]{2,1,0:T(8,128)(2,1)S(1)}, u32[]{:S(2)}) copy-start(bf16[32,128,128]{2,1,0:T(8,128)(2,1)S(1)} %get-tuple-element.25) | copy-start | bytes 3145732
  243.5 6.6 %copy-start.2 = (bf16[48,8,32,128]{3,2,1,0:T(8,128)(2,1)S(1)}, bf16[48,8,32,128]{3,2,1,0:T(8,128)(2,1)}, u32[]{:S(2)}) copy-start(bf16[48,8,32,128]{3,2,1,0:T(8,128)(2,1)} %copy.68) | copy-start | bytes 9437188
  261.9 3.1 copy-start
  261.9 8.9 %slice-start = ((s8[6291456]{0:T(1024)(128)(4,1)}), s8[4194304]{0:T(1024)(128)(4,1)S(1)}, s32[]{:S(2)}) async-start(s8[6291456]{0:T(1024)(128)(4,1)} %bitcast.224), calls=%async_computation.6 | async-start | bytes 8388608
  265.0 5.8 slice-start.1
  273.7 19.5 %copy-start.16 = (bf16[2,128,192]{1,2,0:T(8,128)(2,1)}, bf16[2,128,192]{1,2,0:T(8,128)(2,1)S(1)}, u32[]{:S(2)}) copy-start(bf16[2,128,192]{1,2,0:T(8,128)(2,1)S(1)} %fusion.49) | copy-start | bytes 294916
  289.0 4.2 copy-start.13
  293.2 1.2 copy-start.9
  293.2 1.2 copy-start.21
  293.2 2.5 slice-start.2
  294.5 2.2 slice-start.3
  294.5 2.2 copy-start.26
  306.6 1.4 copy-start.24
  306.6 1.4 copy-start.29
  306.6 1.9 copy-start.4
  317.0 1.0 copy-start.14
  317.0 1.0 copy-start.27
  317.0 295.9 %reduce-scatter.5.cloned.1.call-start = ((), (), s32[]{:S(2)}) async-start(), calls=%async_computation.4 | async-start | bytes 11894784 | tf_op jit(solution)/shard_map/reduce_scatter | solution.py:198
  332.4 6.6 %copy-start.10 = (bf16[2,24,32,8,128]{4,3,2,1,0:T(8,128)(2,1)S(1)}, bf16[2,24,32,8,128]{4,3,2,1,0:T(8,128)(2,1)}, u32[]{:S(2)}) copy-start(bf16[2,24,32,8,128]{4,3,2,1,0:T(8,128)(2,1)} %get-tuple-element.27) | copy-start | bytes 9437188
  332.4 6.6 %copy-start.17 = (bf16[2,128,192]{1,2,0:T(8,128)(2,1)S(1)}, bf16[2,128,192]{1,2,0:T(8,128)(2,1)}, u32[]{:S(2)}) copy-start(bf16[2,128,192]{1,2,0:T(8,128)(2,1)} %copy-done.16) | copy-start | bytes 294916
  343.4 6.3 %copy-start.3 = (bf16[48,8,32,128]{3,2,1,0:T(8,128)(2,1)S(1)}, bf16[48,8,32,128]{3,2,1,0:T(8,128)(2,1)}, u32[]{:S(2)}) copy-start(bf16[48,8,32,128]{3,2,1,0:T(8,128)(2,1)} %copy.68) | copy-start | bytes 9437188
  343.4 6.3 %copy-start.15 = (bf16[2,192,512,1]{2,1,0,3:T(8,128)(2,1)S(1)}, bf16[2,192,512,1]{2,1,0,3:T(8,128)(2,1)}, u32[]{:S(2)}) copy-start(bf16[2,192,512,1]{2,1,0,3:T(8,128)(2,1)} %reshape.232) | copy-start | bytes 1179652
  354.4 101.6 %copy-start.6 = (bf16[32,128,128]{1,2,0:T(8,128)(2,1)S(1)}, bf16[32,128,128]{1,2,0:T(8,128)(2,1)}, u32[]{:S(2)}) copy-start(bf16[32,128,128]{1,2,0:T(8,128)(2,1)} %copy.48) | copy-start | bytes 3145732
  354.4 101.6 %copy-start.7 = (bf16[32,128,128]{1,2,0:T(8,128)(2,1)S(1)}, bf16[32,128,128]{1,2,0:T(8,128)(2,1)}, u32[]{:S(2)}) copy-start(bf16[32,128,128]{1,2,0:T(8,128)(2,1)} %copy.49) | copy-start | bytes 3145732
  475.6 1.2 copy-start.5
  475.6 1.7 copy-start.12
  476.8 1.5 copy-start.11
  476.8 1.5 copy-start.28
  476.8 1.5 copy-start.31
Sparse Core Ops, SparseCore 0:
  13.0 134.9 all-gather.3
  151.2 89.7 all-gather.5
  317.2 133.3 reduce-scatter.2
  475.7 137.0 reduce-scatter.4
